TPU v7x, 32 devices: a whole 2x2x4 slice. The times are simulated.
32 devices in a mesh: band: 4 (over x, core), grid: 8 (over z, y).
Axes of the slice: x: 2, y: 2, z: 4, core: 2. Of those that a mesh axis runs over, the one named last changes fastest.
Arguments:
- orbitals: float32 [4, 128, 128, 128], P('band', 'grid'), may hold values from -4 to 10, as said below
- pivots: int32 [4], replicated, may hold values from 0 to 2097151, as said below
- pattern: int32 [4, 4], replicated, may hold values from 0 to 1, as said below
Outputs:
- localized: float32 [4, 128, 128, 128], P('band', 'grid')
- exchange_term: float32 [4, 128, 128, 128], P('band', 'grid')
Inputs may be any that keep to these rules, and one draw needn't show every extreme that they name: Values of the orbitals on the grid; the matrix of their values at the pivots has a Cholesky factorization. `pivots`: distinct flat cell indices; the first and the last cell of the grid are always among them. `pattern`: every diagonal entry is 1; each row holds 1 to 4 ones, some row exactly 4; the matrix holds exactly 8 ones.
All inputs are finite; a program needn't handle non-finite values.
Results may differ from a plain program's by a relative error of at most 0.0003.
Values sent between devices are 32-bit elements; how exact they have to be, the bound alone decides.
A program may use at most 64 MiB of HBM per device.

v0:
```python
import jax
import jax.numpy as jnp
from jax import lax
from jax.sharding import PartitionSpec as P

MOST_PARTNERS = 4
precise = lax.Precision.HIGHEST


def tables(length):
    across = jnp.arange(length, dtype=jnp.int32)
    phases = across[:, None] * across[None, :] % length
    angles = phases.astype(jnp.float32) * (2.0 * jnp.pi / length)
    return (jnp.cos(angles), jnp.sin(angles))


def wrapped(indices, length):
    return jnp.where(indices < length // 2, indices, indices - length)


def coulomb(length, plane_start, plane_count):
    wave_first = wrapped(jnp.arange(length, dtype=jnp.int32), length).astype(jnp.float32)
    wave_second = wrapped(plane_start + jnp.arange(plane_count, dtype=jnp.int32), length).astype(
        jnp.float32
    )
    squared = (
        wave_first[:, None, None] ** 2
        + wave_second[None, :, None] ** 2
        + wave_first[None, None, :] ** 2
    )
    scaling = float(length) ** 1.5
    return jnp.where(squared > 0, 0.25 / (scaling * jnp.maximum(squared, 1.0)), 0.0)


def densities(first_bands, second_bands):
    return (first_bands[:, None] * second_bands[None, :]).reshape((-1,) + first_bands.shape[1:])


def applied(potential, first_bands, second_bands):
    shaped = potential.reshape(
        (first_bands.shape[0], second_bands.shape[0]) + first_bands.shape[1:]
    )
    return jnp.sum(shaped * second_bands[None], axis=1)


def filtered(real_in, imag_in, kernel, cos_table, sin_table):
    real_part = jnp.dot(real_in, cos_table, precision=precise) + jnp.dot(
        imag_in, sin_table, precision=precise
    )
    imag_part = jnp.dot(imag_in, cos_table, precision=precise) - jnp.dot(
        real_in, sin_table, precision=precise
    )
    real_part, imag_part = (
        jnp.einsum("pxyz,yk->pxkz", real_part, cos_table, precision=precise)
        + jnp.einsum("pxyz,yk->pxkz", imag_part, sin_table, precision=precise),
        jnp.einsum("pxyz,yk->pxkz", imag_part, cos_table, precision=precise)
        - jnp.einsum("pxyz,yk->pxkz", real_part, sin_table, precision=precise),
    )
    real_wide = lax.all_to_all(real_part, "grid", split_axis=2, concat_axis=1, tiled=True)
    imag_wide = lax.all_to_all(imag_part, "grid", split_axis=2, concat_axis=1, tiled=True)
    ahead_real = (
        jnp.einsum("pxyz,xk->pkyz", real_wide, cos_table, precision=precise)
        + jnp.einsum("pxyz,xk->pkyz", imag_wide, sin_table, precision=precise)
    ) * kernel
    ahead_imag = (
        jnp.einsum("pxyz,xk->pkyz", imag_wide, cos_table, precision=precise)
        - jnp.einsum("pxyz,xk->pkyz", real_wide, sin_table, precision=precise)
    ) * kernel
    back_real = jnp.einsum("pxyz,xk->pkyz", ahead_real, cos_table, precision=precise) - jnp.einsum(
        "pxyz,xk->pkyz", ahead_imag, sin_table, precision=precise
    )
    back_imag = jnp.einsum("pxyz,xk->pkyz", ahead_imag, cos_table, precision=precise) + jnp.einsum(
        "pxyz,xk->pkyz", ahead_real, sin_table, precision=precise
    )
    real_part = lax.all_to_all(back_real, "grid", split_axis=1, concat_axis=2, tiled=True)
    imag_part = lax.all_to_all(back_imag, "grid", split_axis=1, concat_axis=2, tiled=True)
    real_part, imag_part = (
        jnp.einsum("pxyz,yk->pxkz", real_part, cos_table, precision=precise)
        - jnp.einsum("pxyz,yk->pxkz", imag_part, sin_table, precision=precise),
        jnp.einsum("pxyz,yk->pxkz", imag_part, cos_table, precision=precise)
        + jnp.einsum("pxyz,yk->pxkz", real_part, sin_table, precision=precise),
    )
    out_real = jnp.dot(real_part, cos_table, precision=precise) - jnp.dot(
        imag_part, sin_table, precision=precise
    )
    out_imag = jnp.dot(imag_part, cos_table, precision=precise) + jnp.dot(
        real_part, sin_table, precision=precise
    )
    return (out_real, out_imag)


def twin_potential(first_one, second_one, first_two, second_two, kernel, cos_table, sin_table):
    potential_one, potential_two = filtered(
        densities(first_one, second_one),
        densities(first_two, second_two),
        kernel,
        cos_table,
        sin_table,
    )
    return (
        applied(potential_one, first_one, second_one),
        applied(potential_two, first_two, second_two),
    )


def collect(wanted, portion):
    positions = jnp.arange(portion.shape[0], dtype=jnp.int32)
    chooser = (wanted[:, None] == positions[None, :]).astype(jnp.float32)
    return jnp.einsum("qm,mxyz->qxyz", chooser, portion, precision=precise)


def local(orbitals, pivots, pattern):
    band_dev = orbitals.shape[0]
    slab_planes = orbitals.shape[1]
    length = orbitals.shape[3]
    block_total = pattern.shape[0]
    grid_index = lax.axis_index("grid")
    band_index = lax.axis_index("band")
    cell_count = slab_planes * length * length
    flat_local = orbitals.reshape(band_dev, cell_count)
    local_cell = pivots - grid_index * cell_count
    inside = (local_cell >= 0) & (local_cell < cell_count)
    sampled = jnp.take(flat_local, jnp.clip(local_cell, 0, cell_count - 1), axis=1)
    partial_pick = jnp.where(inside[None, :], sampled, 0.0)
    own_rows = lax.psum(partial_pick, "grid")
    picked = lax.all_gather(own_rows, "band", axis=0, tiled=True)
    gram_matrix = jnp.dot(picked.T, picked, precision=precise)
    factor = jnp.linalg.cholesky(gram_matrix)
    rotation = lax.linalg.triangular_solve(factor, picked.T, left_side=True, lower=True).T
    own_weights = lax.dynamic_slice_in_dim(rotation, band_index * band_dev, band_dev, 0)
    localized = lax.psum_scatter(
        jnp.einsum("bk,bxyz->kxyz", own_weights, orbitals, precision=precise),
        "band",
        scatter_dimension=0,
        tiled=True,
    )
    cos_table, sin_table = tables(length)
    plane_count = length // lax.axis_size("grid")
    kernel = coulomb(length, grid_index * plane_count, plane_count)
    columns = jnp.arange(block_total, dtype=jnp.int32)
    members = jnp.arange(band_dev, dtype=jnp.int32)
    own_row = lax.dynamic_index_in_dim(pattern, band_index, 0, keepdims=False)
    before = jnp.cumsum(own_row) - own_row
    slot_ids = jnp.arange(MOST_PARTNERS, dtype=jnp.int32)
    matches = (own_row[None, :] == 1) & (before[None, :] == slot_ids[:, None])
    partner = jnp.sum(jnp.where(matches, columns[None, :], 0), axis=1)
    present = jnp.any(matches, axis=1)
    wanted = jnp.where(
        present[:, None], partner[:, None] * band_dev + members[None, :], -1
    ).reshape(-1)
    partners = collect(wanted, lax.all_gather(localized, "band", axis=0, tiled=True))
    exchange_term = jnp.zeros_like(localized)
    for couple in range(MOST_PARTNERS // 2):
        first_rows = partners[2 * couple * band_dev : (2 * couple + 1) * band_dev]
        second_rows = partners[(2 * couple + 1) * band_dev : (2 * couple + 2) * band_dev]
        term_one, term_two = twin_potential(
            localized, first_rows, localized, second_rows, kernel, cos_table, sin_table
        )
        exchange_term = exchange_term + term_one + term_two
    return (localized, exchange_term)


def solution(mesh):
    return jax.shard_map(
        local,
        mesh=mesh,
        in_specs=(P("band", "grid", None, None), P(), P()),
        out_specs=(P("band", "grid", None, None), P("band", "grid", None, None)),
        check_vma=False,
    )
```

profile of v0, /device:TPU:0, one launch (start us, length us, event | category | flops | bytes accessed | tf_op | source)
XLA Modules:
  0.0 410.0 jit_solution(14240325148722384985)
XLA Ops:
  10.0 23.1 %psum.7 = f32[1,4]{1,0:T(1,128)S(1)} all-reduce(f32[1,4]{1,0:T(1,128)S(1)} %fusion.210), channel_id=1, replica_groups=mesh['band'=4,'grid'=8] {'grid'}, use_global_device_ids=true, to_apply=%region_0.1 | all-reduce | flops 4 | bytes 32 | tf_op jit(solution)/shard_map/psum | solution.py:125
  33.1 5.0 %all-gather = f32[4,1,4]{2,1,0:T(1,128)S(1)} all-gather(f32[1,1,4]{2,1,0:T(1,128)S(1)} %bitcast.338), channel_id=1, replica_groups=mesh['band'=4,'grid'=8] {'band'}, dimensions={0}, use_global_device_ids=true | all-gather | bytes 80 | tf_op jit(solution)/shard_map/all_gather | solution.py:126
  40.6 3.8 broadcast_multiply_fusion
  44.4 41.9 %reduce-scatter.2.cloned.1.call-done = f32[1,16,128,128]{3,2,1,0:T(8,128)} async-done(((f32[4,16,128,128]{3,2,1,0:T(8,128)}), f32[1,16,128,128]{3,2,1,0:T(8,128)}) %reduce-scatter.2.cloned.1.call-update) | async-done | bytes 1048592 | tf_op jit(solution)/shard_map/reduce_scatter | solution.py:131
  87.5 35.6 %all-gather.3.cloned.1.call-done = f32[4,16,128,128]{3,2,1,0:T(8,128)} async-done(((f32[1,16,128,128]{3,2,1,0:T(8,128)}), f32[4,16,128,128]{3,2,1,0:T(8,128)}) %all-gather.3.cloned.1.call-update) | async-done | bytes 4194320 | tf_op jit(solution)/shard_map/all_gather | solution.py:151
  123.0 8.5 %fusion = f32[4,16,128,128]{3,0,2,1:T(4,128)S(1)} fusion(f32[4,16,128,128]{3,2,1,0:T(8,128)} %all-gather.3.cloned.1.call-done, s32[4]{0:T(128)S(1)} %broadcast_select_fusion), kind=kOutput, calls=%fused_computation.1 | convolution fusion | flops 50331664 | bytes 8388624 | tf_op jit(solution)/shard_map/qm,mxyz->qxyz/dot_general | solution.py:109
  131.6 3.6 slice_multiply_fusion.3
  145.2 5.8 %all-to-all-start.4 = ((f32[1,16,128,128]{3,1,0,2:T(8,128)}), f32[1,16,128,128]{3,1,0,2:T(8,128)}, u32[]{:S(2)}, u32[]{:S(2)}) async-start(f32[1,16,128,128]{3,1,0,2:T(8,128)} %copy.182), calls=%async_computation.5 | async-start | bytes 2097152 | tf_op jit(solution)/shard_map/all_to_all | solution.py:59
  152.3 2.5 fusion.8
  154.8 1.6 copy.187
  156.4 20.8 %all-to-all-done.4 = f32[1,16,128,128]{3,1,0,2:T(8,128)} async-done(((f32[1,16,128,128]{3,1,0,2:T(8,128)}), f32[1,16,128,128]{3,1,0,2:T(8,128)}, u32[]{:S(2)}, u32[]{:S(2)}) %all-to-all-start.4) | async-done | bytes 1048608 | tf_op jit(solution)/shard_map/all_to_all | solution.py:59
  177.2 4.2 %all-to-all-start.5 = ((f32[1,16,128,128]{3,1,0,2:T(8,128)}), f32[1,16,128,128]{3,1,0,2:T(8,128)}, u32[]{:S(2)}, u32[]{:S(2)}) async-start(f32[1,16,128,128]{3,1,0,2:T(8,128)} %copy.187), calls=%async_computation.6 | async-start | bytes 2097152 | tf_op jit(solution)/shard_map/all_to_all | solution.py:60
  190.5 16.5 %all-to-all-done.5 = f32[1,16,128,128]{3,1,0,2:T(8,128)} async-done(((f32[1,16,128,128]{3,1,0,2:T(8,128)}), f32[1,16,128,128]{3,1,0,2:T(8,128)}, u32[]{:S(2)}, u32[]{:S(2)}) %all-to-all-start.5) | async-done | bytes 1048608 | tf_op jit(solution)/shard_map/all_to_all | solution.py:60
  207.1 4.0 all-to-all-start.1
  213.7 1.6 copy.156
  215.3 21.6 %all-to-all-done.1 = f32[1,16,128,128]{3,1,0,2:T(8,128)S(1)} async-done(((f32[1,16,128,128]{3,1,0,2:T(8,128)}), f32[1,16,128,128]{3,1,0,2:T(8,128)S(1)}, u32[]{:S(2)}, u32[]{:S(2)}) %all-to-all-start.1) | async-done | bytes 1048608 | tf_op jit(solution)/shard_map/all_to_all | solution.py:60
  236.8 3.6 all-to-all-start
  251.4 1.6 copy.194
  253.0 13.5 %all-to-all-done = f32[1,16,128,128]{3,1,0,2:T(8,128)S(1)} async-done(((f32[1,16,128,128]{3,1,0,2:T(8,128)}), f32[1,16,128,128]{3,1,0,2:T(8,128)S(1)}, u32[]{:S(2)}, u32[]{:S(2)}) %all-to-all-start) | async-done | bytes 1048608 | tf_op jit(solution)/shard_map/all_to_all | solution.py:59
  267.4 3.8 all-to-all-start.6
  273.8 1.6 copy.199
  275.4 21.8 %all-to-all-done.6 = f32[1,128,16,128]{3,2,0,1:T(8,128)S(1)} async-done(((f32[1,128,16,128]{3,2,0,1:T(8,128)}), f32[1,128,16,128]{3,2,0,1:T(8,128)S(1)}, u32[]{:S(2)}, u32[]{:S(2)}) %all-to-all-start.6) | async-done | bytes 1048608 | tf_op jit(solution)/shard_map/all_to_all | solution.py:75
  297.2 4.2 %all-to-all-start.7 = ((f32[1,128,16,128]{3,2,0,1:T(8,128)}), f32[1,128,16,128]{3,2,0,1:T(8,128)}, u32[]{:S(2)}, u32[]{:S(2)}) async-start(f32[1,128,16,128]{3,2,0,1:T(8,128)} %copy.199), calls=%async_computation.8 | async-start | bytes 2097152 | tf_op jit(solution)/shard_map/all_to_all | solution.py:76
  309.8 1.6 copy.173
  311.4 15.6 %all-to-all-done.7 = f32[1,128,16,128]{3,2,0,1:T(8,128)} async-done(((f32[1,128,16,128]{3,2,0,1:T(8,128)}), f32[1,128,16,128]{3,2,0,1:T(8,128)}, u32[]{:S(2)}, u32[]{:S(2)}) %all-to-all-start.7) | async-done | bytes 1048608 | tf_op jit(solution)/shard_map/all_to_all | solution.py:76
  327.1 4.6 %all-to-all-start.3 = ((f32[1,128,16,128]{3,2,0,1:T(8,128)}), f32[1,128,16,128]{3,2,0,1:T(8,128)}, u32[]{:S(2)}, u32[]{:S(2)}) async-start(f32[1,128,16,128]{3,2,0,1:T(8,128)} %copy.173), calls=%async_computation.4 | async-start | bytes 2097152 | tf_op jit(solution)/shard_map/all_to_all | solution.py:76
  334.3 1.6 copy.168
  337.3 2.3 fusion.48
  339.6 17.5 %all-to-all-done.3 = f32[1,128,16,128]{3,2,0,1:T(8,128)} async-done(((f32[1,128,16,128]{3,2,0,1:T(8,128)}), f32[1,128,16,128]{3,2,0,1:T(8,128)}, u32[]{:S(2)}, u32[]{:S(2)}) %all-to-all-start.3) | async-done | bytes 1048608 | tf_op jit(solution)/shard_map/all_to_all | solution.py:76
  357.1 4.2 %all-to-all-start.2 = ((f32[1,128,16,128]{3,2,0,1:T(8,128)}), f32[1,128,16,128]{3,2,0,1:T(8,128)}, u32[]{:S(2)}, u32[]{:S(2)}) async-start(f32[1,128,16,128]{3,2,0,1:T(8,128)} %copy.168), calls=%async_computation.3 | async-start | bytes 2097152 | tf_op jit(solution)/shard_map/all_to_all | solution.py:75
  371.6 15.2 %all-to-all-done.2 = f32[1,128,16,128]{3,2,0,1:T(8,128)} async-done(((f32[1,128,16,128]{3,2,0,1:T(8,128)}), f32[1,128,16,128]{3,2,0,1:T(8,128)}, u32[]{:S(2)}, u32[]{:S(2)}) %all-to-all-start.2) | async-done | bytes 1048608 | tf_op jit(solution)/shard_map/all_to_all | solution.py:75
  398.4 4.5 %multiply_add_fusion = f32[1,16,128,128]{3,0,2,1:T(1,128)} fusion(f32[1,16,128,128]{3,0,2,1:T(1,128)S(1)} %bitcast.318, f32[1,16,128,128]{3,0,2,1:T(1,128)S(1)} %bitcast.317, f32[1,16,128,128]{3,0,2,1:T(1,128)S(1)} %bitcast.319, f32[1,16,128,128]{3,0,2,1:T(1,128)S(1)} %bitcast.320, f32[4,16,128,128]{3,0,2,1:T(4,128)S(1)} %copy-done.1), kind=kLoop, calls=%fused_computation.49 | loop fusion | flops 1835008 | bytes 9437184 | tf_op jit(solution)/shard_map/add | solution.py:159
  (101 shorter events, 77.8 us)
Async XLA Ops:
  7.2 79.1 %reduce-scatter.2.cloned.1.call-start = ((), (), s32[]{:S(2)}) async-start(), calls=%async_computation.9 | async-start | bytes 5242880 | tf_op jit(solution)/shard_map/reduce_scatter | solution.py:131
  44.4 78.6 %all-gather.3.cloned.1.call-start = ((), (), s32[]{:S(2)}) async-start(), calls=%async_computation.10 | async-start | bytes 5242880 | tf_op jit(solution)/shard_map/all_gather | solution.py:151
  87.5 44.1 %copy-start.3 = (f32[1,16,128,128]{3,2,1,0:T(8,128)S(1)}, f32[1,16,128,128]{3,2,1,0:T(8,128)}, u32[]{:S(2)}) copy-start(f32[1,16,128,128]{3,2,1,0:T(8,128)} %reduce-scatter.2.cloned.1.call-done) | copy-start | bytes 3145732
  131.6 3.6 copy-start
  140.1 1.0 copy-start.2
  145.2 32.0 %all-to-all-start.4 = ((f32[1,16,128,128]{3,1,0,2:T(8,128)}), f32[1,16,128,128]{3,1,0,2:T(8,128)}, u32[]{:S(2)}, u32[]{:S(2)}) async-start(f32[1,16,128,128]{3,1,0,2:T(8,128)} %copy.182), calls=%async_computation.5 | async-start | bytes 2097152 | tf_op jit(solution)/shard_map/all_to_all | solution.py:59
  177.2 29.9 %all-to-all-start.5 = ((f32[1,16,128,128]{3,1,0,2:T(8,128)}), f32[1,16,128,128]{3,1,0,2:T(8,128)}, u32[]{:S(2)}, u32[]{:S(2)}) async-start(f32[1,16,128,128]{3,1,0,2:T(8,128)} %copy.187), calls=%async_computation.6 | async-start | bytes 2097152 | tf_op jit(solution)/shard_map/all_to_all | solution.py:60
  207.1 29.7 %all-to-all-start.1 = ((f32[1,16,128,128]{3,1,0,2:T(8,128)}), f32[1,16,128,128]{3,1,0,2:T(8,128)S(1)}, u32[]{:S(2)}, u32[]{:S(2)}) async-start(f32[1,16,128,128]{3,1,0,2:T(8,128)} %copy.161), calls=%async_computation.2 | async-start | bytes 2097152 | tf_op jit(solution)/shard_map/all_to_all | solution.py:60
  236.8 7.7 %copy-start.5 = (f32[1,16,128,128]{3,1,0,2:T(8,128)}, f32[1,16,128,128]{3,1,0,2:T(8,128)S(1)}, u32[]{:S(2)}) copy-start(f32[1,16,128,128]{3,1,0,2:T(8,128)S(1)} %all-to-all-done.1) | copy-start | bytes 3145732
  236.8 29.6 %all-to-all-start = ((f32[1,16,128,128]{3,1,0,2:T(8,128)}), f32[1,16,128,128]{3,1,0,2:T(8,128)S(1)}, u32[]{:S(2)}, u32[]{:S(2)}) async-start(f32[1,16,128,128]{3,1,0,2:T(8,128)} %copy.156), calls=%async_computation.1 | async-start | bytes 2097152 | tf_op jit(solution)/shard_map/all_to_all | solution.py:59
  266.4 1.0 copy-start.7
  267.4 29.8 %all-to-all-start.6 = ((f32[1,128,16,128]{3,2,0,1:T(8,128)}), f32[1,128,16,128]{3,2,0,1:T(8,128)S(1)}, u32[]{:S(2)}, u32[]{:S(2)}) async-start(f32[1,128,16,128]{3,2,0,1:T(8,128)} %copy.194), calls=%async_computation.7 | async-start | bytes 2097152 | tf_op jit(solution)/shard_map/all_to_all | solution.py:75
  272.5 28.9 %copy-start.6 = (f32[1,16,128,128]{3,1,0,2:T(8,128)S(1)}, f32[1,16,128,128]{3,1,0,2:T(8,128)}, u32[]{:S(2)}) copy-start(f32[1,16,128,128]{3,1,0,2:T(8,128)} %copy-done.5) | copy-start | bytes 3145732
  273.8 27.7 %copy-start.8 = (f32[1,16,128,128]{3,1,0,2:T(8,128)S(1)}, f32[1,16,128,128]{3,1,0,2:T(8,128)}, u32[]{:S(2)}) copy-start(f32[1,16,128,128]{3,1,0,2:T(8,128)} %copy-done.7) | copy-start | bytes 3145732
  297.2 29.9 %all-to-all-start.7 = ((f32[1,128,16,128]{3,2,0,1:T(8,128)}), f32[1,128,16,128]{3,2,0,1:T(8,128)}, u32[]{:S(2)}, u32[]{:S(2)}) async-start(f32[1,128,16,128]{3,2,0,1:T(8,128)} %copy.199), calls=%async_computation.8 | async-start | bytes 2097152 | tf_op jit(solution)/shard_map/all_to_all | solution.py:76
  327.1 30.1 %all-to-all-start.3 = ((f32[1,128,16,128]{3,2,0,1:T(8,128)}), f32[1,128,16,128]{3,2,0,1:T(8,128)}, u32[]{:S(2)}, u32[]{:S(2)}) async-start(f32[1,128,16,128]{3,2,0,1:T(8,128)} %copy.173), calls=%async_computation.4 | async-start | bytes 2097152 | tf_op jit(solution)/shard_map/all_to_all | solution.py:76
  357.1 29.7 %all-to-all-start.2 = ((f32[1,128,16,128]{3,2,0,1:T(8,128)}), f32[1,128,16,128]{3,2,0,1:T(8,128)}, u32[]{:S(2)}, u32[]{:S(2)}) async-start(f32[1,128,16,128]{3,2,0,1:T(8,128)} %copy.168), calls=%async_computation.3 | async-start | bytes 2097152 | tf_op jit(solution)/shard_map/all_to_all | solution.py:75
  362.7 4.0 copy-start.4
  394.7 3.7 copy-start.1
Sparse Core Ops, SparseCore 0:
  44.5 41.7 reduce-scatter.1
  88.5 34.4 all-gather.2
where the time goes:
time: 417 us; the launch traced here: 410 us
  waiting for transfers between devices  220 us (53%)
  matrix products  72.7 us (17%)
  starting transfers between devices  34.7 us (8%)
  blocking collectives  28.1 us (7%)
  local copies, waits for them, and re-layouts  23.3 us (6%)
  other arithmetic  16.4 us (4%)
  between operations  14.9 us (4%)
    reduce_scatter x1, waiting for transfers between devices, local(): lax.psum_scatter(jnp.einsum('bk,bxyz->kxyz', own_weights, orbitals, preci...  41.9 us
    all_to_all x2, waiting for transfers between devices, filtered(): lax.all_to_all(imag_part, 'grid', split_axis=2, concat_axis=1, tiled=True)  38.1 us
    all_to_all x2, waiting for transfers between devices, filtered(): lax.all_to_all(back_real, 'grid', split_axis=1, concat_axis=2, tiled=True)  36.9 us
    all_gather x1, waiting for transfers between devices, local(): lax.all_gather(localized, 'band', axis=0, tiled=True)  35.6 us
    all_to_all x2, waiting for transfers between devices, filtered(): lax.all_to_all(real_part, 'grid', split_axis=2, concat_axis=1, tiled=True)  34.3 us
    all_to_all x2, waiting for transfers between devices, filtered(): lax.all_to_all(back_imag, 'grid', split_axis=1, concat_axis=2, tiled=True)  33.2 us
    psum x1, blocking collectives, local(): own_rows = lax.psum(partial_pick, 'grid')  23.1 us
    all_to_all x2, starting transfers between devices, filtered(): lax.all_to_all(real_part, 'grid', split_axis=2, concat_axis=1, tiled=True)  9.43 us
  transfers between devices with their start and end apart: 10, of which 10 were waited for; matrix products, arithmetic and copies ran while one was open for 16% of the time, Pallas kernels for 0%

commit v1 on v0

--- a/solution.py
+++ b/solution.py
@@ -1,3 +1,4 @@
+import functools
 import jax
 import jax.numpy as jnp
 from jax import lax
@@ -5,6 +6,17 @@
 
 MOST_PARTNERS = 4
 precise = lax.Precision.HIGHEST
+
+
+def _change_point(xin, dim_k, dimension_no):
+    w2 = lax.axis_size("grid")
+    small = jnp.split(xin, w2, axis=dim_k)
+    right_arr = jnp.stack(small)
+    local_part = lax.all_to_all(right_arr, "grid", 0, 0)
+    return jnp.concatenate(local_part, axis=dimension_no)
+
+
+lots_all_take = functools.partial(_change_point, dim_k=2, dimension_no=1)
 
 
 def tables(length):
@@ -56,7 +68,7 @@
         jnp.einsum("pxyz,yk->pxkz", imag_part, cos_table, precision=precise)
         - jnp.einsum("pxyz,yk->pxkz", real_part, sin_table, precision=precise),
     )
-    real_wide = lax.all_to_all(real_part, "grid", split_axis=2, concat_axis=1, tiled=True)
+    real_wide = lots_all_take(real_part)
     imag_wide = lax.all_to_all(imag_part, "grid", split_axis=2, concat_axis=1, tiled=True)
     ahead_real = (
         jnp.einsum("pxyz,xk->pkyz", real_wide, cos_table, precision=precise)

time: 417 us -> 418 us (level)
  waiting for transfers between devices: 220 us -> 213 us
  local copies, waits for them, and re-layouts: 23.3 us -> 29.4 us
    unnamed x18 -> x30, local copies, waits for them, and re-layouts: 1.98 us -> 10.2 us
    all_to_all x2, waiting for transfers between devices: 34.3 us -> 28.3 us  [_change_point(): local_part = lax.all_to_all(right_arr, 'grid', 0, 0)]
    all_to_all x2, waiting for transfers between devices: 33.2 us -> 28.1 us  [filtered(): lax.all_to_all(back_imag, 'grid', split_axis=1, concat_axis=2, tiled=True)]
  transfers between devices with their start and end apart: 10 -> 10, of which waited for: 10 -> 10; matrix products, arithmetic and copies ran while one was open for 16% -> 17% of each run, Pallas kernels for 0% -> 0%
where the time goes in v1:
time: 418 us; the launch traced here: 412 us
  waiting for transfers between devices  213 us (51%)
  matrix products  74.8 us (18%)
  starting transfers between devices  34.6 us (8%)
  local copies, waits for them, and re-layouts  29.4 us (7%)
  blocking collectives  28.1 us (7%)
  other arithmetic  16.4 us (4%)
  between operations  14.9 us (4%)
    reduce_scatter x1, waiting for transfers between devices, local(): lax.psum_scatter(jnp.einsum('bk,bxyz->kxyz', own_weights, orbitals, preci...  41.9 us
    all_to_all x2, waiting for transfers between devices, filtered(): lax.all_to_all(imag_part, 'grid', split_axis=2, concat_axis=1, tiled=True)  41.6 us
    all_to_all x2, waiting for transfers between devices, filtered(): lax.all_to_all(back_real, 'grid', split_axis=1, concat_axis=2, tiled=True)  37.9 us
    all_gather x1, waiting for transfers between devices, local(): lax.all_gather(localized, 'band', axis=0, tiled=True)  35.5 us
    all_to_all x2, waiting for transfers between devices, _change_point(): local_part = lax.all_to_all(right_arr, 'grid', 0, 0)  28.3 us
    all_to_all x2, waiting for transfers between devices, filtered(): lax.all_to_all(back_imag, 'grid', split_axis=1, concat_axis=2, tiled=True)  28.1 us
    psum x1, blocking collectives, local(): own_rows = lax.psum(partial_pick, 'grid')  23.1 us
    unnamed x30, local copies, waits for them, and re-layouts  10.2 us
  transfers between devices with their start and end apart: 10, of which 10 were waited for; matrix products, arithmetic and copies ran while one was open for 17% of the time, Pallas kernels for 0%

profile of v1, /device:TPU:0, one launch (start us, length us, event | category | flops | bytes accessed | tf_op | source)
XLA Modules:
  0.0 411.6 jit_solution(15783216000196142425)
XLA Ops:
  10.0 23.1 %psum.7 = f32[1,4]{1,0:T(1,128)S(1)} all-reduce(f32[1,4]{1,0:T(1,128)S(1)} %fusion.230), channel_id=1, replica_groups=mesh['band'=4,'grid'=8] {'grid'}, use_global_device_ids=true, to_apply=%region_0.1 | all-reduce | flops 4 | bytes 32 | tf_op jit(solution)/shard_map/psum | solution.py:137
  33.1 5.0 %all-gather = f32[4,1,4]{2,1,0:T(1,128)S(1)} all-gather(f32[1,1,4]{2,1,0:T(1,128)S(1)} %bitcast.389), channel_id=1, replica_groups=mesh['band'=4,'grid'=8] {'band'}, dimensions={0}, use_global_device_ids=true | all-gather | bytes 80 | tf_op jit(solution)/shard_map/all_gather | solution.py:138
  40.6 3.8 broadcast_multiply_fusion
  44.4 41.9 %reduce-scatter.2.cloned.1.call-done = f32[1,16,128,128]{3,2,1,0:T(8,128)} async-done(((f32[4,16,128,128]{3,2,1,0:T(8,128)}), f32[1,16,128,128]{3,2,1,0:T(8,128)}) %reduce-scatter.2.cloned.1.call-update) | async-done | bytes 1048592 | tf_op jit(solution)/shard_map/reduce_scatter | solution.py:143
  87.5 35.5 %all-gather.3.cloned.1.call-done = f32[4,16,128,128]{3,2,1,0:T(8,128)} async-done(((f32[1,16,128,128]{3,2,1,0:T(8,128)}), f32[4,16,128,128]{3,2,1,0:T(8,128)}) %all-gather.3.cloned.1.call-update) | async-done | bytes 4194320 | tf_op jit(solution)/shard_map/all_gather | solution.py:163
  123.0 8.5 %fusion = f32[4,16,128,128]{3,0,2,1:T(4,128)S(1)} fusion(f32[4,16,128,128]{3,2,1,0:T(8,128)} %all-gather.3.cloned.1.call-done, s32[4]{0:T(128)S(1)} %broadcast_select_fusion), kind=kOutput, calls=%fused_computation.1 | convolution fusion | flops 50331664 | bytes 8388624 | tf_op jit(solution)/shard_map/qm,mxyz->qxyz/dot_general | solution.py:121
  131.6 3.6 slice_multiply_fusion.3
  145.3 1.6 copy.190
  146.8 5.8 %all-to-all-start.5 = ((f32[1,16,128,128]{3,1,0,2:T(8,128)}), f32[1,16,128,128]{3,1,0,2:T(8,128)}, u32[]{:S(2)}, u32[]{:S(2)}) async-start(f32[1,16,128,128]{3,1,0,2:T(8,128)} %copy.190), calls=%async_computation.6 | async-start | bytes 2097152 | tf_op jit(solution)/shard_map/all_to_all | solution.py:72
  157.9 20.9 %all-to-all-done.5 = f32[1,16,128,128]{3,1,0,2:T(8,128)} async-done(((f32[1,16,128,128]{3,1,0,2:T(8,128)}), f32[1,16,128,128]{3,1,0,2:T(8,128)}, u32[]{:S(2)}, u32[]{:S(2)}) %all-to-all-start.5) | async-done | bytes 1048608 | tf_op jit(solution)/shard_map/all_to_all | solution.py:72
  178.8 3.6 all-to-all-start.4
  190.0 1.6 copy.164
  194.2 14.2 %all-to-all-done.4 = f32[8,1,16,16,128]{4,3,2,1,0:T(8,128)S(1)} async-done(((f32[8,1,16,16,128]{4,3,2,1,0:T(8,128)}), f32[8,1,16,16,128]{4,3,2,1,0:T(8,128)S(1)}, u32[]{:S(2)}, u32[]{:S(2)}) %all-to-all-start.4) | async-done | bytes 1048608 | tf_op jit(solution)/shard_map/all_to_all | solution.py:15
  209.4 3.6 all-to-all-start.1
  218.3 20.7 %all-to-all-done.1 = f32[1,16,128,128]{3,1,0,2:T(8,128)S(1)} async-done(((f32[1,16,128,128]{3,1,0,2:T(8,128)}), f32[1,16,128,128]{3,1,0,2:T(8,128)S(1)}, u32[]{:S(2)}, u32[]{:S(2)}) %all-to-all-start.1) | async-done | bytes 1048608 | tf_op jit(solution)/shard_map/all_to_all | solution.py:72
  239.0 4.6 %all-to-all-start = ((f32[8,1,16,16,128]{4,3,2,1,0:T(8,128)}), f32[8,1,16,16,128]{4,3,2,1,0:T(8,128)}, u32[]{:S(2)}, u32[]{:S(2)}) async-start(f32[8,1,16,16,128]{4,3,2,1,0:T(8,128)} %fusion.35), calls=%async_computation.1 | async-start | bytes 2097152 | tf_op jit(solution)/shard_map/all_to_all | solution.py:15
  250.7 1.7 fusion.6
  253.6 1.6 copy.198
  255.2 14.1 %all-to-all-done = f32[8,1,16,16,128]{4,3,2,1,0:T(8,128)} async-done(((f32[8,1,16,16,128]{4,3,2,1,0:T(8,128)}), f32[8,1,16,16,128]{4,3,2,1,0:T(8,128)}, u32[]{:S(2)}, u32[]{:S(2)}) %all-to-all-start) | async-done | bytes 1048608 | tf_op jit(solution)/shard_map/all_to_all | solution.py:15
  269.3 4.4 %all-to-all-start.6 = ((f32[1,128,16,128]{3,2,0,1:T(8,128)}), f32[1,128,16,128]{3,2,0,1:T(8,128)}, u32[]{:S(2)}, u32[]{:S(2)}) async-start(f32[1,128,16,128]{3,2,0,1:T(8,128)} %copy.198), calls=%async_computation.7 | async-start | bytes 2097152 | tf_op jit(solution)/shard_map/all_to_all | solution.py:87
  277.9 21.3 %all-to-all-done.6 = f32[1,128,16,128]{3,2,0,1:T(8,128)} async-done(((f32[1,128,16,128]{3,2,0,1:T(8,128)}), f32[1,128,16,128]{3,2,0,1:T(8,128)}, u32[]{:S(2)}, u32[]{:S(2)}) %all-to-all-start.6) | async-done | bytes 1048608 | tf_op jit(solution)/shard_map/all_to_all | solution.py:87
  299.1 4.2 %all-to-all-start.7 = ((f32[1,128,16,128]{3,2,0,1:T(8,128)}), f32[1,128,16,128]{3,2,0,1:T(8,128)}, u32[]{:S(2)}, u32[]{:S(2)}) async-start(f32[1,128,16,128]{3,2,0,1:T(8,128)} %copy.203), calls=%async_computation.8 | async-start | bytes 2097152 | tf_op jit(solution)/shard_map/all_to_all | solution.py:88
  304.8 2.7 fusion.25
  310.3 2.9 fusion.14
  314.5 1.6 copy.172
  316.1 12.7 %all-to-all-done.7 = f32[1,128,16,128]{3,2,0,1:T(8,128)} async-done(((f32[1,128,16,128]{3,2,0,1:T(8,128)}), f32[1,128,16,128]{3,2,0,1:T(8,128)}, u32[]{:S(2)}, u32[]{:S(2)}) %all-to-all-start.7) | async-done | bytes 1048608 | tf_op jit(solution)/shard_map/all_to_all | solution.py:88
  328.8 4.0 all-to-all-start.2
  339.6 2.3 fusion.70
  341.9 16.6 %all-to-all-done.2 = f32[1,128,16,128]{3,2,0,1:T(8,128)S(1)} async-done(((f32[1,128,16,128]{3,2,0,1:T(8,128)}), f32[1,128,16,128]{3,2,0,1:T(8,128)S(1)}, u32[]{:S(2)}, u32[]{:S(2)}) %all-to-all-start.2) | async-done | bytes 1048608 | tf_op jit(solution)/shard_map/all_to_all | solution.py:87
  358.5 4.2 %all-to-all-start.3 = ((f32[1,128,16,128]{3,2,0,1:T(8,128)}), f32[1,128,16,128]{3,2,0,1:T(8,128)}, u32[]{:S(2)}, u32[]{:S(2)}) async-start(f32[1,128,16,128]{3,2,0,1:T(8,128)} %copy.177), calls=%async_computation.4 | async-start | bytes 2097152 | tf_op jit(solution)/shard_map/all_to_all | solution.py:88
  373.0 15.4 %all-to-all-done.3 = f32[1,128,16,128]{3,2,0,1:T(8,128)} async-done(((f32[1,128,16,128]{3,2,0,1:T(8,128)}), f32[1,128,16,128]{3,2,0,1:T(8,128)}, u32[]{:S(2)}, u32[]{:S(2)}) %all-to-all-start.3) | async-done | bytes 1048608 | tf_op jit(solution)/shard_map/all_to_all | solution.py:88
  400.0 4.5 %multiply_add_fusion = f32[1,16,128,128]{3,0,2,1:T(1,128)} fusion(f32[1,16,128,128]{3,0,2,1:T(1,128)S(1)} %bitcast.372, f32[1,16,128,128]{3,0,2,1:T(1,128)S(1)} %bitcast.371, f32[1,16,128,128]{3,0,2,1:T(1,128)S(1)} %bitcast.374, f32[1,16,128,128]{3,0,2,1:T(1,128)S(1)} %bitcast.373, f32[4,16,128,128]{3,0,2,1:T(4,128)S(1)} %copy-done.1), kind=kLoop, calls=%fused_computation.49 | loop fusion | flops 1835008 | bytes 9437184 | tf_op jit(solution)/shard_map/add | solution.py:171
  (111 shorter events, 84.4 us)
Async XLA Ops:
  7.2 79.2 %reduce-scatter.2.cloned.1.call-start = ((), (), s32[]{:S(2)}) async-start(), calls=%async_computation.9 | async-start | bytes 5242880 | tf_op jit(solution)/shard_map/reduce_scatter | solution.py:143
  44.4 78.6 %all-gather.3.cloned.1.call-start = ((), (), s32[]{:S(2)}) async-start(), calls=%async_computation.10 | async-start | bytes 5242880 | tf_op jit(solution)/shard_map/all_gather | solution.py:163
  87.5 44.1 %copy-start.2 = (f32[1,16,128,128]{3,2,1,0:T(8,128)S(1)}, f32[1,16,128,128]{3,2,1,0:T(8,128)}, u32[]{:S(2)}) copy-start(f32[1,16,128,128]{3,2,1,0:T(8,128)} %reduce-scatter.2.cloned.1.call-done) | copy-start | bytes 3145732
  131.6 3.6 copy-start
  146.8 32.0 %all-to-all-start.5 = ((f32[1,16,128,128]{3,1,0,2:T(8,128)}), f32[1,16,128,128]{3,1,0,2:T(8,128)}, u32[]{:S(2)}, u32[]{:S(2)}) async-start(f32[1,16,128,128]{3,1,0,2:T(8,128)} %copy.190), calls=%async_computation.6 | async-start | bytes 2097152 | tf_op jit(solution)/shard_map/all_to_all | solution.py:72
  178.8 29.6 %all-to-all-start.4 = ((f32[8,1,16,16,128]{4,3,2,1,0:T(8,128)}), f32[8,1,16,16,128]{4,3,2,1,0:T(8,128)S(1)}, u32[]{:S(2)}, u32[]{:S(2)}) async-start(f32[8,1,16,16,128]{4,3,2,1,0:T(8,128)} %fusion.27), calls=%async_computation.5 | async-start | bytes 2097152 | tf_op jit(solution)/shard_map/all_to_all | solution.py:15
  208.4 1.0 copy-start.4
  209.4 29.6 %all-to-all-start.1 = ((f32[1,16,128,128]{3,1,0,2:T(8,128)}), f32[1,16,128,128]{3,1,0,2:T(8,128)S(1)}, u32[]{:S(2)}, u32[]{:S(2)}) async-start(f32[1,16,128,128]{3,1,0,2:T(8,128)} %copy.164), calls=%async_computation.2 | async-start | bytes 2097152 | tf_op jit(solution)/shard_map/all_to_all | solution.py:72
  213.0 33.3 %copy-start.5 = (f32[8,1,16,16,128]{4,3,2,1,0:T(8,128)S(1)}, f32[8,1,16,16,128]{4,3,2,1,0:T(8,128)}, u32[]{:S(2)}) copy-start(f32[8,1,16,16,128]{4,3,2,1,0:T(8,128)} %copy-done.4) | copy-start | bytes 3145732
  239.0 30.3 %all-to-all-start = ((f32[8,1,16,16,128]{4,3,2,1,0:T(8,128)}), f32[8,1,16,16,128]{4,3,2,1,0:T(8,128)}, u32[]{:S(2)}, u32[]{:S(2)}) async-start(f32[8,1,16,16,128]{4,3,2,1,0:T(8,128)} %fusion.35), calls=%async_computation.1 | async-start | bytes 2097152 | tf_op jit(solution)/shard_map/all_to_all | solution.py:15
  247.9 2.8 copy-start.6
  269.3 29.8 %all-to-all-start.6 = ((f32[1,128,16,128]{3,2,0,1:T(8,128)}), f32[1,128,16,128]{3,2,0,1:T(8,128)}, u32[]{:S(2)}, u32[]{:S(2)}) async-start(f32[1,128,16,128]{3,2,0,1:T(8,128)} %copy.198), calls=%async_computation.7 | async-start | bytes 2097152 | tf_op jit(solution)/shard_map/all_to_all | solution.py:87
  299.1 29.7 %all-to-all-start.7 = ((f32[1,128,16,128]{3,2,0,1:T(8,128)}), f32[1,128,16,128]{3,2,0,1:T(8,128)}, u32[]{:S(2)}, u32[]{:S(2)}) async-start(f32[1,128,16,128]{3,2,0,1:T(8,128)} %copy.203), calls=%async_computation.8 | async-start | bytes 2097152 | tf_op jit(solution)/shard_map/all_to_all | solution.py:88
  328.8 29.7 %all-to-all-start.2 = ((f32[1,128,16,128]{3,2,0,1:T(8,128)}), f32[1,128,16,128]{3,2,0,1:T(8,128)S(1)}, u32[]{:S(2)}, u32[]{:S(2)}) async-start(f32[1,128,16,128]{3,2,0,1:T(8,128)} %copy.172), calls=%async_computation.3 | async-start | bytes 2097152 | tf_op jit(solution)/shard_map/all_to_all | solution.py:87
  358.5 5.5 %copy-start.7 = (f32[1,128,16,128]{3,2,0,1:T(8,128)}, f32[1,128,16,128]{3,2,0,1:T(8,128)S(1)}, u32[]{:S(2)}) copy-start(f32[1,128,16,128]{3,2,0,1:T(8,128)S(1)} %all-to-all-done.2) | copy-start | bytes 3145732
  358.5 29.9 %all-to-all-start.3 = ((f32[1,128,16,128]{3,2,0,1:T(8,128)}), f32[1,128,16,128]{3,2,0,1:T(8,128)}, u32[]{:S(2)}, u32[]{:S(2)}) async-start(f32[1,128,16,128]{3,2,0,1:T(8,128)} %copy.177), calls=%async_computation.4 | async-start | bytes 2097152 | tf_op jit(solution)/shard_map/all_to_all | solution.py:88
  364.0 4.0 copy-start.3
  396.3 3.7 copy-start.1
Sparse Core Ops, SparseCore 0:
  44.5 41.7 reduce-scatter.1
  88.5 34.4 all-gather.2
